TPU v7x, 32 devices: a whole 2x2x4 slice. The times are simulated.
32 devices in a mesh: gx: 4 (over y, x), gy: 8 (over z, core).
Axes of the slice: x: 2, y: 2, z: 4, core: 2. Of those that a mesh axis runs over, the one named last changes fastest.
Arguments:
- probes: float32 [24, 48, 64, 128], P('gx', 'gy'), may hold values from -6 to 6
- pair_blocks: float32 [24, 48, 9, 128, 128], P('gx', 'gy'), may hold values from -0.09375 to 0.09375
- partners: int32 [24, 48, 9], P('gx', 'gy'), may hold values from 0 to 1151, as said below
- shifts: int32 [2, 24, 48, 9], P(None, 'gx', 'gy'), may hold values from -1 to 1, as said below
- counts: int32 [24, 48], P('gx', 'gy'), may hold values from 1 to 9, as said below
- kpoint: float32 [2], replicated, may hold values from -3.140625 to 3.140625
Outputs:
- last_vector: float32 [24, 48, 64, 128], P('gx', 'gy')
- intersections: float32 [3, 2, 32], replicated
Inputs may be any that keep to these rules, and one draw needn't show every extreme that they name: `partners`: slot 0 of cell (x, y) names the cell itself; slots 1 to 8 name its eight neighbouring cells (x + dx, y + dy) with dx, dy in -1..1 taken periodically modulo 24 and 48, each once, in no fixed order. shifts[0, x, y, s] = (x + dx - px) / 24 and shifts[1, x, y, s] = (y + dy - py) / 48 for the slot's offset (dx, dy) and partner cell (px, py). `counts`: slots at or beyond a cell's count are padding; some cell has all 9 slots live.
All inputs are finite; a program needn't handle non-finite values.
Results may differ from a plain program's by a relative error of at most 0.0001.
Values sent between devices are 32-bit elements; how exact they have to be, the bound alone decides.
A program may use at most 128 MiB of HBM per device.

v0:
```python
import math

import jax
import jax.numpy as jnp
from jax import lax
from jax.sharding import PartitionSpec as P

STEPS = 3


def with_halo(cells, sides, width):
    for axis, dim in sides:
        count = lax.axis_size(axis)
        head = lax.slice_in_dim(cells, 0, width, axis=dim)
        tail = lax.slice_in_dim(cells, cells.shape[dim] - width, cells.shape[dim], axis=dim)
        cells = jnp.concatenate(
            [
                lax.ppermute(tail, axis, [(i, (i + 1) % count) for i in range(count)]),
                cells,
                lax.ppermute(head, axis, [((i + 1) % count, i) for i in range(count)]),
            ],
            axis=dim,
        )
    return cells


def intersection(first, other):
    half = first.shape[2] // 2
    first_re, first_im = (first[:, :, :half], first[:, :, half:])
    other_re, other_im = (other[:, :, :half], other[:, :, half:])
    real_part = jnp.sum(first_re * other_re + first_im * other_im, axis=(0, 1, 3))
    imag_part = jnp.sum(first_re * other_im - first_im * other_re, axis=(0, 1, 3))
    return jnp.stack([real_part, imag_part])


def extend(field):
    return with_halo(field, (("gx", 0), ("gy", 1)), 1)


def shards(probes, pair_blocks, partners, shifts, counts, kpoint):
    cells_x, cells_y, width, block = probes.shape
    slot_total = pair_blocks.shape[2]
    half = width // 2
    cells = cells_x * cells_y
    total_x = cells_x * lax.axis_size("gx")
    total_y = cells_y * lax.axis_size("gy")
    start_x = lax.axis_index("gx") * cells_x
    start_y = lax.axis_index("gy") * cells_y
    partner_x = partners // total_y
    partner_y = partners % total_y
    local_x = jnp.mod(partner_x - start_x + 1, total_x)
    local_y = jnp.mod(partner_y - start_y + 1, total_y)
    flat_partner = (local_x * (cells_y + 2) + local_y).reshape(cells, slot_total)
    angle = kpoint[0] * shifts[0].astype(jnp.float32) + kpoint[1] * shifts[1].astype(jnp.float32)
    angle = angle.reshape(cells, slot_total)
    live = (jnp.arange(slot_total, dtype=jnp.int32)[None, :] < counts.reshape(cells, 1)).astype(
        jnp.float32
    )
    cosine = jnp.cos(angle) * live
    sine = jnp.sin(angle) * live
    blocks = pair_blocks.reshape(cells, slot_total, block, block)
    slot_bound = jnp.max(counts)

    def apply_hamiltonian(field):
        source = extend(field).reshape(-1, width, block)

        def accumulate(slot, sums):
            real_sum, imag_sum = sums
            piece = jnp.take(source, flat_partner[:, slot], axis=0)
            chosen = lax.dynamic_index_in_dim(blocks, slot, 1, keepdims=False)
            product = jnp.einsum("npb,nba->npa", piece, chosen, precision=lax.Precision.HIGHEST)
            cos_part = lax.dynamic_index_in_dim(cosine, slot, 1, keepdims=False)[:, None, None]
            sin_part = lax.dynamic_index_in_dim(sine, slot, 1, keepdims=False)[:, None, None]
            real_part = product[:, :half]
            imag_part = product[:, half:]
            return (
                real_sum + cos_part * real_part - sin_part * imag_part,
                imag_sum + sin_part * real_part + cos_part * imag_part,
            )

        zeros = jnp.zeros((cells, half, block), jnp.float32)
        real_sum, imag_sum = lax.fori_loop(0, slot_bound, accumulate, (zeros, zeros))
        return jnp.concatenate([real_sum, imag_sum], axis=1).reshape(field.shape)

    scale = 1.0 / math.sqrt(total_x * total_y * block)

    def reduce_one(field):
        return lax.psum(intersection(probes, field), ("gx", "gy")) * scale

    before = probes
    current = apply_hamiltonian(probes)
    partial_list = []
    partial_list.append(reduce_one(current))
    for step in range(STEPS - 1):
        following = 2.0 * apply_hamiltonian(current) - before
        before, current = (current, following)
        partial_list.append(reduce_one(current))
    found = jnp.stack(partial_list)
    return (current, found)


def solution(mesh):
    placed = (
        P("gx", "gy", None, None),
        P("gx", "gy", None, None, None),
        P("gx", "gy", None),
        P(None, "gx", "gy", None),
        P("gx", "gy"),
        P(),
    )
    return jax.shard_map(
        shards,
        mesh=mesh,
        in_specs=placed,
        out_specs=(P("gx", "gy", None, None), P()),
        check_vma=False,
    )
```

profile of v0, /device:TPU:0, one launch (start us, length us, event | category | flops | bytes accessed | tf_op | source)
XLA Modules:
  0.0 336.4 jit_solution(18082595083658992762)
XLA Ops:
  0.6 1.1 fusion.46
  1.8 3.0 collective-permute-start
  4.8 1.0 collective-permute-start.1
  5.8 1.3 fusion.47
  7.1 2.8 sine_reduce_fusion
  11.6 3.5 %collective-permute-done.1 = f32[1,6,64,128]{3,2,1,0:T(8,128)S(1)} collective-permute-done((f32[1,6,64,128]{3,2,1,0:T(8,128)S(1)}, f32[1,6,64,128]{3,2,1,0:T(8,128)S(1)}, u32[]{:S(2)}, u32[]{:S(2)}) %collective-permute-start.1) | collective-permute-done | bytes 196640 | tf_op jit(solution)/shard_map/ppermute | solution.py:20
  15.2 1.2 copy-done.21
  16.5 3.5 %collective-permute-start.3 = (f32[8,1,64,128]{3,2,1,0:T(8,128)S(1)}, f32[8,1,64,128]{3,2,1,0:T(8,128)S(1)}, u32[]{:S(2)}, u32[]{:S(2)}) collective-permute-start(f32[8,1,64,128]{3,2,1,0:T(8,128)S(1)} %get-tuple-element.273), channel_id=1, source_target_pairs={{1,0},{2,1},{3,2},{4,3},{5,4},{6,5},{7,6},{0,7},{9,8},{10,9},{11,1... | collective-permute-start | bytes 786440 | tf_op jit(solution)/shard_map/ppermute | solution.py:20
  20.4 15.5 %copy.12 = f32[6,6,9,128,128]{4,3,1,0,2:T(8,128)} copy(f32[6,6,9,128,128]{4,3,2,1,0:T(8,128)} %param.15) | data formatting | bytes 42467328 | tf_op args[1]
  36.5 1.6 pad_maximum_fusion
  38.1 0.9 broadcast.33.clone.3
  39.9 67.6 %while.36 = (s32[]{:T(128)}, f32[36,32,128]{2,1,0:T(8,128)}, f32[36,32,128]{2,1,0:T(8,128)}, s32[]{:T(128)}, f32[36,9]{0,1:T(8,128)S(1)}, /*index=5*/s32[36,9]{0...) while((s32[]{:T(128)}, f32[36,32,128]{2,1,0:T(8,128)}, ...), condition=%wide.region_2.4_spmd, body=%wide.region_1.3_spmd.sunk | while | flops 454460640 | bytes 20059900 | solution.py:82
  41.2 4.0 %fusion.62 = f32[36,64,128]{2,1,0:T(8,128)S(1)} fusion(f32[36,9,128,128]{3,2,0,1:T(8,128)} %get-tuple-element.523, s32[]{:T(128)S(6)} %select_n.106, f32[36,64,128]{2,1,0:T(8,128)S(1)} %gather_fusion, pred[36]{0:T(512)(128)(4,1)S(1)} %get-tuple-element.457), kind=kOutput, calls=%fused_computation.3.clone.1 | convolution fusion | flops 453279744 | bytes 4718632 | tf_op jit(solution)/shard_map/while/body/npb,nba->npa/dot_general | solution.py:71
  48.7 4.0 %fusion.62 = f32[36,64,128]{2,1,0:T(8,128)S(1)} fusion(f32[36,9,128,128]{3,2,0,1:T(8,128)} %get-tuple-element.523, s32[]{:T(128)S(6)} %select_n.106, f32[36,64,128]{2,1,0:T(8,128)S(1)} %gather_fusion, pred[36]{0:T(512)(128)(4,1)S(1)} %get-tuple-element.457), kind=kOutput, calls=%fused_computation.3.clone.1 | convolution fusion | flops 453279744 | bytes 4718632 | tf_op jit(solution)/shard_map/while/body/npb,nba->npa/dot_general | solution.py:71
  56.1 4.0 %fusion.62 = f32[36,64,128]{2,1,0:T(8,128)S(1)} fusion(f32[36,9,128,128]{3,2,0,1:T(8,128)} %get-tuple-element.523, s32[]{:T(128)S(6)} %select_n.106, f32[36,64,128]{2,1,0:T(8,128)S(1)} %gather_fusion, pred[36]{0:T(512)(128)(4,1)S(1)} %get-tuple-element.457), kind=kOutput, calls=%fused_computation.3.clone.1 | convolution fusion | flops 453279744 | bytes 4718632 | tf_op jit(solution)/shard_map/while/body/npb,nba->npa/dot_general | solution.py:71
  63.5 4.0 %fusion.62 = f32[36,64,128]{2,1,0:T(8,128)S(1)} fusion(f32[36,9,128,128]{3,2,0,1:T(8,128)} %get-tuple-element.523, s32[]{:T(128)S(6)} %select_n.106, f32[36,64,128]{2,1,0:T(8,128)S(1)} %gather_fusion, pred[36]{0:T(512)(128)(4,1)S(1)} %get-tuple-element.457), kind=kOutput, calls=%fused_computation.3.clone.1 | convolution fusion | flops 453279744 | bytes 4718632 | tf_op jit(solution)/shard_map/while/body/npb,nba->npa/dot_general | solution.py:71
  71.0 4.0 %fusion.62 = f32[36,64,128]{2,1,0:T(8,128)S(1)} fusion(f32[36,9,128,128]{3,2,0,1:T(8,128)} %get-tuple-element.523, s32[]{:T(128)S(6)} %select_n.106, f32[36,64,128]{2,1,0:T(8,128)S(1)} %gather_fusion, pred[36]{0:T(512)(128)(4,1)S(1)} %get-tuple-element.457), kind=kOutput, calls=%fused_computation.3.clone.1 | convolution fusion | flops 453279744 | bytes 4718632 | tf_op jit(solution)/shard_map/while/body/npb,nba->npa/dot_general | solution.py:71
  78.4 4.0 %fusion.62 = f32[36,64,128]{2,1,0:T(8,128)S(1)} fusion(f32[36,9,128,128]{3,2,0,1:T(8,128)} %get-tuple-element.523, s32[]{:T(128)S(6)} %select_n.106, f32[36,64,128]{2,1,0:T(8,128)S(1)} %gather_fusion, pred[36]{0:T(512)(128)(4,1)S(1)} %get-tuple-element.457), kind=kOutput, calls=%fused_computation.3.clone.1 | convolution fusion | flops 453279744 | bytes 4718632 | tf_op jit(solution)/shard_map/while/body/npb,nba->npa/dot_general | solution.py:71
  85.9 4.0 %fusion.62 = f32[36,64,128]{2,1,0:T(8,128)S(1)} fusion(f32[36,9,128,128]{3,2,0,1:T(8,128)} %get-tuple-element.523, s32[]{:T(128)S(6)} %select_n.106, f32[36,64,128]{2,1,0:T(8,128)S(1)} %gather_fusion, pred[36]{0:T(512)(128)(4,1)S(1)} %get-tuple-element.457), kind=kOutput, calls=%fused_computation.3.clone.1 | convolution fusion | flops 453279744 | bytes 4718632 | tf_op jit(solution)/shard_map/while/body/npb,nba->npa/dot_general | solution.py:71
  93.3 4.0 %fusion.62 = f32[36,64,128]{2,1,0:T(8,128)S(1)} fusion(f32[36,9,128,128]{3,2,0,1:T(8,128)} %get-tuple-element.523, s32[]{:T(128)S(6)} %select_n.106, f32[36,64,128]{2,1,0:T(8,128)S(1)} %gather_fusion, pred[36]{0:T(512)(128)(4,1)S(1)} %get-tuple-element.457), kind=kOutput, calls=%fused_computation.3.clone.1 | convolution fusion | flops 453279744 | bytes 4718632 | tf_op jit(solution)/shard_map/while/body/npb,nba->npa/dot_general | solution.py:71
  100.7 4.0 %fusion.62 = f32[36,64,128]{2,1,0:T(8,128)S(1)} fusion(f32[36,9,128,128]{3,2,0,1:T(8,128)} %get-tuple-element.523, s32[]{:T(128)S(6)} %select_n.106, f32[36,64,128]{2,1,0:T(8,128)S(1)} %gather_fusion, pred[36]{0:T(512)(128)(4,1)S(1)} %get-tuple-element.457), kind=kOutput, calls=%fused_computation.3.clone.1 | convolution fusion | flops 453279744 | bytes 4718632 | tf_op jit(solution)/shard_map/while/body/npb,nba->npa/dot_general | solution.py:71
  107.5 1.2 constant_dynamic-update-slice_fusion.4
  108.8 1.5 collective-permute-start.4
  110.4 1.4 collective-permute-start.5
  111.8 3.6 %collective-permute-done.4 = f32[1,6,64,128]{3,2,1,0:T(8,128)S(1)} collective-permute-done((f32[1,6,64,128]{3,2,1,0:T(8,128)S(1)}, f32[1,6,64,128]{3,2,1,0:T(8,128)S(1)}, u32[]{:S(2)}, u32[]{:S(2)}) %collective-permute-start.4) | collective-permute-done | bytes 196640 | tf_op jit(solution)/shard_map/ppermute | solution.py:18
  115.4 2.5 collective-permute-done.5
  118.8 3.5 %collective-permute-start.7 = (f32[8,1,64,128]{3,2,1,0:T(8,128)S(1)}, f32[8,1,64,128]{3,2,1,0:T(8,128)}, u32[]{:S(2)}, u32[]{:S(2)}) collective-permute-start(f32[8,1,64,128]{3,2,1,0:T(8,128)S(1)} %get-tuple-element.271), channel_id=1, source_target_pairs={{1,0},{2,1},{3,2},{4,3},{5,4},{6,5},{7,6},{0,7},{9,8},{10,9},{11,1... | collective-permute-start | bytes 786440 | tf_op jit(solution)/shard_map/ppermute | solution.py:20
  122.3 6.1 %collective-permute-done.6 = f32[8,1,64,128]{3,2,1,0:T(8,128)S(1)} collective-permute-done((f32[8,1,64,128]{3,2,1,0:T(8,128)S(1)}, f32[8,1,64,128]{3,2,1,0:T(8,128)S(1)}, u32[]{:S(2)}, u32[]{:S(2)}) %collective-permute-start.6) | collective-permute-done | bytes 262176 | tf_op jit(solution)/shard_map/ppermute | solution.py:18
  129.1 1.3 pad_maximum_fusion.1
  130.5 0.9 broadcast.33.clone.1
  131.3 0.9 broadcast.33.clone.2
  132.2 67.6 %while.37 = (s32[]{:T(128)}, f32[36,32,128]{2,1,0:T(8,128)}, f32[36,32,128]{2,1,0:T(8,128)}, s32[]{:T(128)}, f32[36,9]{0,1:T(8,128)S(1)}, /*index=5*/s32[36,9]{0...) while((s32[]{:T(128)}, f32[36,32,128]{2,1,0:T(8,128)}, ...), condition=%wide.region_4.6_spmd, body=%wide.region_3.5_spmd.sunk | while | flops 454460640 | bytes 20059900 | solution.py:82
  133.6 4.0 %fusion.66 = f32[36,64,128]{2,1,0:T(8,128)S(1)} fusion(f32[36,9,128,128]{3,2,0,1:T(8,128)} %get-tuple-element.559, s32[]{:T(128)S(6)} %select_n.108, f32[36,64,128]{2,1,0:T(8,128)S(1)} %gather_fusion.1, pred[36]{0:T(512)(128)(4,1)S(1)} %get-tuple-element.472), kind=kOutput, calls=%fused_computation.22.clone.1 | convolution fusion | flops 453279744 | bytes 4718632 | tf_op jit(solution)/shard_map/while/body/npb,nba->npa/dot_general | solution.py:71
  141.0 4.0 %fusion.66 = f32[36,64,128]{2,1,0:T(8,128)S(1)} fusion(f32[36,9,128,128]{3,2,0,1:T(8,128)} %get-tuple-element.559, s32[]{:T(128)S(6)} %select_n.108, f32[36,64,128]{2,1,0:T(8,128)S(1)} %gather_fusion.1, pred[36]{0:T(512)(128)(4,1)S(1)} %get-tuple-element.472), kind=kOutput, calls=%fused_computation.22.clone.1 | convolution fusion | flops 453279744 | bytes 4718632 | tf_op jit(solution)/shard_map/while/body/npb,nba->npa/dot_general | solution.py:71
  148.5 4.0 %fusion.66 = f32[36,64,128]{2,1,0:T(8,128)S(1)} fusion(f32[36,9,128,128]{3,2,0,1:T(8,128)} %get-tuple-element.559, s32[]{:T(128)S(6)} %select_n.108, f32[36,64,128]{2,1,0:T(8,128)S(1)} %gather_fusion.1, pred[36]{0:T(512)(128)(4,1)S(1)} %get-tuple-element.472), kind=kOutput, calls=%fused_computation.22.clone.1 | convolution fusion | flops 453279744 | bytes 4718632 | tf_op jit(solution)/shard_map/while/body/npb,nba->npa/dot_general | solution.py:71
  155.9 4.0 %fusion.66 = f32[36,64,128]{2,1,0:T(8,128)S(1)} fusion(f32[36,9,128,128]{3,2,0,1:T(8,128)} %get-tuple-element.559, s32[]{:T(128)S(6)} %select_n.108, f32[36,64,128]{2,1,0:T(8,128)S(1)} %gather_fusion.1, pred[36]{0:T(512)(128)(4,1)S(1)} %get-tuple-element.472), kind=kOutput, calls=%fused_computation.22.clone.1 | convolution fusion | flops 453279744 | bytes 4718632 | tf_op jit(solution)/shard_map/while/body/npb,nba->npa/dot_general | solution.py:71
  163.3 4.0 %fusion.66 = f32[36,64,128]{2,1,0:T(8,128)S(1)} fusion(f32[36,9,128,128]{3,2,0,1:T(8,128)} %get-tuple-element.559, s32[]{:T(128)S(6)} %select_n.108, f32[36,64,128]{2,1,0:T(8,128)S(1)} %gather_fusion.1, pred[36]{0:T(512)(128)(4,1)S(1)} %get-tuple-element.472), kind=kOutput, calls=%fused_computation.22.clone.1 | convolution fusion | flops 453279744 | bytes 4718632 | tf_op jit(solution)/shard_map/while/body/npb,nba->npa/dot_general | solution.py:71
  170.8 4.0 %fusion.66 = f32[36,64,128]{2,1,0:T(8,128)S(1)} fusion(f32[36,9,128,128]{3,2,0,1:T(8,128)} %get-tuple-element.559, s32[]{:T(128)S(6)} %select_n.108, f32[36,64,128]{2,1,0:T(8,128)S(1)} %gather_fusion.1, pred[36]{0:T(512)(128)(4,1)S(1)} %get-tuple-element.472), kind=kOutput, calls=%fused_computation.22.clone.1 | convolution fusion | flops 453279744 | bytes 4718632 | tf_op jit(solution)/shard_map/while/body/npb,nba->npa/dot_general | solution.py:71
  178.2 4.0 %fusion.66 = f32[36,64,128]{2,1,0:T(8,128)S(1)} fusion(f32[36,9,128,128]{3,2,0,1:T(8,128)} %get-tuple-element.559, s32[]{:T(128)S(6)} %select_n.108, f32[36,64,128]{2,1,0:T(8,128)S(1)} %gather_fusion.1, pred[36]{0:T(512)(128)(4,1)S(1)} %get-tuple-element.472), kind=kOutput, calls=%fused_computation.22.clone.1 | convolution fusion | flops 453279744 | bytes 4718632 | tf_op jit(solution)/shard_map/while/body/npb,nba->npa/dot_general | solution.py:71
  185.6 4.0 %fusion.66 = f32[36,64,128]{2,1,0:T(8,128)S(1)} fusion(f32[36,9,128,128]{3,2,0,1:T(8,128)} %get-tuple-element.559, s32[]{:T(128)S(6)} %select_n.108, f32[36,64,128]{2,1,0:T(8,128)S(1)} %gather_fusion.1, pred[36]{0:T(512)(128)(4,1)S(1)} %get-tuple-element.472), kind=kOutput, calls=%fused_computation.22.clone.1 | convolution fusion | flops 453279744 | bytes 4718632 | tf_op jit(solution)/shard_map/while/body/npb,nba->npa/dot_general | solution.py:71
  193.1 4.0 %fusion.66 = f32[36,64,128]{2,1,0:T(8,128)S(1)} fusion(f32[36,9,128,128]{3,2,0,1:T(8,128)} %get-tuple-element.559, s32[]{:T(128)S(6)} %select_n.108, f32[36,64,128]{2,1,0:T(8,128)S(1)} %gather_fusion.1, pred[36]{0:T(512)(128)(4,1)S(1)} %get-tuple-element.472), kind=kOutput, calls=%fused_computation.22.clone.1 | convolution fusion | flops 453279744 | bytes 4718632 | tf_op jit(solution)/shard_map/while/body/npb,nba->npa/dot_general | solution.py:71
  199.8 1.4 maximum_multiply_fusion
  201.7 2.9 collective-permute-start.9
  204.7 3.6 %collective-permute-done.8 = f32[1,6,64,128]{3,2,1,0:T(8,128)S(1)} collective-permute-done((f32[1,6,64,128]{3,2,1,0:T(8,128)S(1)}, f32[1,6,64,128]{3,2,1,0:T(8,128)S(1)}, u32[]{:S(2)}, u32[]{:S(2)}) %collective-permute-start.8) | collective-permute-done | bytes 196640 | tf_op jit(solution)/shard_map/ppermute | solution.py:18
  208.3 4.1 %collective-permute-done.9 = f32[1,6,64,128]{3,2,1,0:T(8,128)S(1)} collective-permute-done((f32[1,6,64,128]{3,2,1,0:T(8,128)S(1)}, f32[1,6,64,128]{3,2,1,0:T(8,128)S(1)}, u32[]{:S(2)}, u32[]{:S(2)}) %collective-permute-start.9) | collective-permute-done | bytes 196640 | tf_op jit(solution)/shard_map/ppermute | solution.py:20
  213.2 3.5 %collective-permute-start.11 = (f32[8,1,64,128]{3,2,1,0:T(8,128)S(1)}, f32[8,1,64,128]{3,2,1,0:T(8,128)}, u32[]{:S(2)}, u32[]{:S(2)}) collective-permute-start(f32[8,1,64,128]{3,2,1,0:T(8,128)S(1)} %get-tuple-element.269), channel_id=1, source_target_pairs={{1,0},{2,1},{3,2},{4,3},{5,4},{6,5},{7,6},{0,7},{9,8},{10,9},{11,1... | collective-permute-start | bytes 786440 | tf_op jit(solution)/shard_map/ppermute | solution.py:20
  216.7 5.6 %collective-permute-done.10 = f32[8,1,64,128]{3,2,1,0:T(8,128)S(1)} collective-permute-done((f32[8,1,64,128]{3,2,1,0:T(8,128)S(1)}, f32[8,1,64,128]{3,2,1,0:T(8,128)S(1)}, u32[]{:S(2)}, u32[]{:S(2)}) %collective-permute-start.10) | collective-permute-done | bytes 262176 | tf_op jit(solution)/shard_map/ppermute | solution.py:18
  223.0 1.3 pad_maximum_fusion.2
  224.4 0.9 broadcast.33
  225.3 0.9 broadcast.33.clone
  226.2 68.2 %while.38 = (s32[]{:T(128)}, f32[36,32,128]{2,1,0:T(8,128)}, f32[36,32,128]{2,1,0:T(8,128)}, s32[]{:T(128)}, f32[36,9]{0,1:T(8,128)S(1)}, /*index=5*/s32[36,9]{0...) while((s32[]{:T(128)}, f32[36,32,128]{2,1,0:T(8,128)}, ...), condition=%wide.region_6.8_spmd, body=%wide.region_5.7_spmd.sunk | while | flops 454460640 | bytes 20059900 | solution.py:82
  227.7 4.0 %fusion.70 = f32[36,64,128]{2,1,0:T(8,128)S(1)} fusion(f32[36,9,128,128]{3,2,0,1:T(8,128)} %get-tuple-element.595, s32[]{:T(128)S(6)} %select_n.110, f32[36,64,128]{2,1,0:T(8,128)S(1)} %gather_fusion.2, pred[36]{0:T(512)(128)(4,1)S(1)} %get-tuple-element.487), kind=kOutput, calls=%fused_computation.41.clone.1 | convolution fusion | flops 453279744 | bytes 4718632 | tf_op jit(solution)/shard_map/while/body/npb,nba->npa/dot_general | solution.py:71
  235.2 4.0 %fusion.70 = f32[36,64,128]{2,1,0:T(8,128)S(1)} fusion(f32[36,9,128,128]{3,2,0,1:T(8,128)} %get-tuple-element.595, s32[]{:T(128)S(6)} %select_n.110, f32[36,64,128]{2,1,0:T(8,128)S(1)} %gather_fusion.2, pred[36]{0:T(512)(128)(4,1)S(1)} %get-tuple-element.487), kind=kOutput, calls=%fused_computation.41.clone.1 | convolution fusion | flops 453279744 | bytes 4718632 | tf_op jit(solution)/shard_map/while/body/npb,nba->npa/dot_general | solution.py:71
  242.7 4.0 %fusion.70 = f32[36,64,128]{2,1,0:T(8,128)S(1)} fusion(f32[36,9,128,128]{3,2,0,1:T(8,128)} %get-tuple-element.595, s32[]{:T(128)S(6)} %select_n.110, f32[36,64,128]{2,1,0:T(8,128)S(1)} %gather_fusion.2, pred[36]{0:T(512)(128)(4,1)S(1)} %get-tuple-element.487), kind=kOutput, calls=%fused_computation.41.clone.1 | convolution fusion | flops 453279744 | bytes 4718632 | tf_op jit(solution)/shard_map/while/body/npb,nba->npa/dot_general | solution.py:71
  250.2 4.0 %fusion.70 = f32[36,64,128]{2,1,0:T(8,128)S(1)} fusion(f32[36,9,128,128]{3,2,0,1:T(8,128)} %get-tuple-element.595, s32[]{:T(128)S(6)} %select_n.110, f32[36,64,128]{2,1,0:T(8,128)S(1)} %gather_fusion.2, pred[36]{0:T(512)(128)(4,1)S(1)} %get-tuple-element.487), kind=kOutput, calls=%fused_computation.41.clone.1 | convolution fusion | flops 453279744 | bytes 4718632 | tf_op jit(solution)/shard_map/while/body/npb,nba->npa/dot_general | solution.py:71
  257.7 4.0 %fusion.70 = f32[36,64,128]{2,1,0:T(8,128)S(1)} fusion(f32[36,9,128,128]{3,2,0,1:T(8,128)} %get-tuple-element.595, s32[]{:T(128)S(6)} %select_n.110, f32[36,64,128]{2,1,0:T(8,128)S(1)} %gather_fusion.2, pred[36]{0:T(512)(128)(4,1)S(1)} %get-tuple-element.487), kind=kOutput, calls=%fused_computation.41.clone.1 | convolution fusion | flops 453279744 | bytes 4718632 | tf_op jit(solution)/shard_map/while/body/npb,nba->npa/dot_general | solution.py:71
  265.1 4.0 %fusion.70 = f32[36,64,128]{2,1,0:T(8,128)S(1)} fusion(f32[36,9,128,128]{3,2,0,1:T(8,128)} %get-tuple-element.595, s32[]{:T(128)S(6)} %select_n.110, f32[36,64,128]{2,1,0:T(8,128)S(1)} %gather_fusion.2, pred[36]{0:T(512)(128)(4,1)S(1)} %get-tuple-element.487), kind=kOutput, calls=%fused_computation.41.clone.1 | convolution fusion | flops 453279744 | bytes 4718632 | tf_op jit(solution)/shard_map/while/body/npb,nba->npa/dot_general | solution.py:71
  272.6 4.0 %fusion.70 = f32[36,64,128]{2,1,0:T(8,128)S(1)} fusion(f32[36,9,128,128]{3,2,0,1:T(8,128)} %get-tuple-element.595, s32[]{:T(128)S(6)} %select_n.110, f32[36,64,128]{2,1,0:T(8,128)S(1)} %gather_fusion.2, pred[36]{0:T(512)(128)(4,1)S(1)} %get-tuple-element.487), kind=kOutput, calls=%fused_computation.41.clone.1 | convolution fusion | flops 453279744 | bytes 4718632 | tf_op jit(solution)/shard_map/while/body/npb,nba->npa/dot_general | solution.py:71
  280.1 4.0 %fusion.70 = f32[36,64,128]{2,1,0:T(8,128)S(1)} fusion(f32[36,9,128,128]{3,2,0,1:T(8,128)} %get-tuple-element.595, s32[]{:T(128)S(6)} %select_n.110, f32[36,64,128]{2,1,0:T(8,128)S(1)} %gather_fusion.2, pred[36]{0:T(512)(128)(4,1)S(1)} %get-tuple-element.487), kind=kOutput, calls=%fused_computation.41.clone.1 | convolution fusion | flops 453279744 | bytes 4718632 | tf_op jit(solution)/shard_map/while/body/npb,nba->npa/dot_general | solution.py:71
  287.6 4.0 %fusion.70 = f32[36,64,128]{2,1,0:T(8,128)S(1)} fusion(f32[36,9,128,128]{3,2,0,1:T(8,128)} %get-tuple-element.595, s32[]{:T(128)S(6)} %select_n.110, f32[36,64,128]{2,1,0:T(8,128)S(1)} %gather_fusion.2, pred[36]{0:T(512)(128)(4,1)S(1)} %get-tuple-element.487), kind=kOutput, calls=%fused_computation.41.clone.1 | convolution fusion | flops 453279744 | bytes 4718632 | tf_op jit(solution)/shard_map/while/body/npb,nba->npa/dot_general | solution.py:71
  294.4 1.4 maximum_multiply_fusion.1
  296.2 1.1 copy-done.16
  297.6 1.2 add_reduce_fusion.2
  298.9 36.9 %all-reduce = (f32[2,32]{1,0:T(2,128)S(1)}, f32[2,32]{1,0:T(2,128)S(1)}, f32[2,32]{1,0:T(2,128)S(1)}) all-reduce(f32[2,32]{1,0:T(2,128)S(1)} %pad_maximum_fusion.12, f32[2,32]{1,0:T(2,128)S(1)} %pad_maximum_fusion.11, f32[2,32]{1,0:T(2,128)S(1)} %pad_maximum_fusion.10), channel_id=1, replica_groups=mesh['gx'=4,'gy'=8] {'gx','gy'}, use_global_device_ids=true, to_apply=%region_15.17 | all-reduce | flops 192 | bytes 1536 | tf_op jit(solution)/shard_map/psum | solution.py:88
  (418 shorter events, 81.9 us)
Async XLA Ops:
  0.6 10.9 %copy-start.17 = (f32[6,6,64,128]{3,2,1,0:T(8,128)S(1)}, f32[6,6,64,128]{3,2,1,0:T(8,128)}, u32[]{:S(2)}) copy-start(f32[6,6,64,128]{3,2,1,0:T(8,128)} %param.14) | copy-start | bytes 3538948
  1.8 9.7 %collective-permute-start = (f32[1,6,64,128]{3,2,1,0:T(8,128)S(1)}, f32[1,6,64,128]{3,2,1,0:T(8,128)S(1)}, u32[]{:S(2)}, u32[]{:S(2)}) collective-permute-start(f32[1,6,64,128]{3,2,1,0:T(8,128)S(1)} %get-tuple-element.281), channel_id=1, source_target_pairs={{0,8},{8,16},{16,24},{24,0},{1,9},{9,17},{17,25},{25,1},{2,10},{10... | collective-permute-start | bytes 589832 | tf_op jit(solution)/shard_map/ppermute | solution.py:18
  4.8 10.3 %collective-permute-start.1 = (f32[1,6,64,128]{3,2,1,0:T(8,128)S(1)}, f32[1,6,64,128]{3,2,1,0:T(8,128)S(1)}, u32[]{:S(2)}, u32[]{:S(2)}) collective-permute-start(f32[1,6,64,128]{3,2,1,0:T(8,128)S(1)} %get-tuple-element.280), channel_id=1, source_target_pairs={{8,0},{16,8},{24,16},{0,24},{9,1},{17,9},{25,17},{1,25},{10,2},{18... | collective-permute-start | bytes 589832 | tf_op jit(solution)/shard_map/ppermute | solution.py:20
  11.6 8.6 %copy-start.26 = (s32[6,6,9]{2,1,0:T(8,128)S(1)}, s32[6,6,9]{2,1,0:T(8,128)}, u32[]{:S(2)}) copy-start(s32[6,6,9]{2,1,0:T(8,128)} %param.16) | copy-start | bytes 3892
  16.4 20.1 %collective-permute-start.2 = (f32[8,1,64,128]{3,2,1,0:T(8,128)S(1)}, f32[8,1,64,128]{3,2,1,0:T(8,128)S(1)}, u32[]{:S(2)}, u32[]{:S(2)}) collective-permute-start(f32[8,1,64,128]{3,2,1,0:T(8,128)S(1)} %get-tuple-element.272), channel_id=1, source_target_pairs={{0,1},{1,2},{2,3},{3,4},{4,5},{5,6},{6,7},{7,0},{8,9},{9,10},{10,1... | collective-permute-start | bytes 786440 | tf_op jit(solution)/shard_map/ppermute | solution.py:18
  16.5 20.1 %collective-permute-start.3 = (f32[8,1,64,128]{3,2,1,0:T(8,128)S(1)}, f32[8,1,64,128]{3,2,1,0:T(8,128)S(1)}, u32[]{:S(2)}, u32[]{:S(2)}) collective-permute-start(f32[8,1,64,128]{3,2,1,0:T(8,128)S(1)} %get-tuple-element.273), channel_id=1, source_target_pairs={{1,0},{2,1},{3,2},{4,3},{5,4},{6,5},{7,6},{0,7},{9,8},{10,9},{11,1... | collective-permute-start | bytes 786440 | tf_op jit(solution)/shard_map/ppermute | solution.py:20
  20.4 15.5 %copy-start.27 = (s32[6,6]{1,0:T(8,128)S(1)}, s32[6,6]{1,0:T(8,128)}, u32[]{:S(2)}) copy-start(s32[6,6]{1,0:T(8,128)} %param.18) | copy-start | bytes 436
  41.2 4.1 %copy-start.4 = (f32[36,32,128]{2,1,0:T(8,128)S(1)}, f32[36,32,128]{2,1,0:T(8,128)}, u32[]{:S(2)}) copy-start(f32[36,32,128]{2,1,0:T(8,128)} %get-tuple-element.505) | copy-start | bytes 1769476 | tf_op jit(solution)/shard_map/while
  41.2 4.1 %copy-start.6 = (f32[36,32,128]{2,1,0:T(8,128)S(1)}, f32[36,32,128]{2,1,0:T(8,128)}, u32[]{:S(2)}) copy-start(f32[36,32,128]{2,1,0:T(8,128)} %get-tuple-element.506) | copy-start | bytes 1769476 | tf_op jit(solution)/shard_map/while
  48.6 4.1 %copy-start.4 = (f32[36,32,128]{2,1,0:T(8,128)S(1)}, f32[36,32,128]{2,1,0:T(8,128)}, u32[]{:S(2)}) copy-start(f32[36,32,128]{2,1,0:T(8,128)} %get-tuple-element.505) | copy-start | bytes 1769476 | tf_op jit(solution)/shard_map/while
  48.6 4.1 %copy-start.6 = (f32[36,32,128]{2,1,0:T(8,128)S(1)}, f32[36,32,128]{2,1,0:T(8,128)}, u32[]{:S(2)}) copy-start(f32[36,32,128]{2,1,0:T(8,128)} %get-tuple-element.506) | copy-start | bytes 1769476 | tf_op jit(solution)/shard_map/while
  56.1 4.1 %copy-start.4 = (f32[36,32,128]{2,1,0:T(8,128)S(1)}, f32[36,32,128]{2,1,0:T(8,128)}, u32[]{:S(2)}) copy-start(f32[36,32,128]{2,1,0:T(8,128)} %get-tuple-element.505) | copy-start | bytes 1769476 | tf_op jit(solution)/shard_map/while
  56.1 4.1 %copy-start.6 = (f32[36,32,128]{2,1,0:T(8,128)S(1)}, f32[36,32,128]{2,1,0:T(8,128)}, u32[]{:S(2)}) copy-start(f32[36,32,128]{2,1,0:T(8,128)} %get-tuple-element.506) | copy-start | bytes 1769476 | tf_op jit(solution)/shard_map/while
  63.5 4.1 %copy-start.4 = (f32[36,32,128]{2,1,0:T(8,128)S(1)}, f32[36,32,128]{2,1,0:T(8,128)}, u32[]{:S(2)}) copy-start(f32[36,32,128]{2,1,0:T(8,128)} %get-tuple-element.505) | copy-start | bytes 1769476 | tf_op jit(solution)/shard_map/while
  63.5 4.1 %copy-start.6 = (f32[36,32,128]{2,1,0:T(8,128)S(1)}, f32[36,32,128]{2,1,0:T(8,128)}, u32[]{:S(2)}) copy-start(f32[36,32,128]{2,1,0:T(8,128)} %get-tuple-element.506) | copy-start | bytes 1769476 | tf_op jit(solution)/shard_map/while
  71.0 4.1 %copy-start.4 = (f32[36,32,128]{2,1,0:T(8,128)S(1)}, f32[36,32,128]{2,1,0:T(8,128)}, u32[]{:S(2)}) copy-start(f32[36,32,128]{2,1,0:T(8,128)} %get-tuple-element.505) | copy-start | bytes 1769476 | tf_op jit(solution)/shard_map/while
  71.0 4.1 %copy-start.6 = (f32[36,32,128]{2,1,0:T(8,128)S(1)}, f32[36,32,128]{2,1,0:T(8,128)}, u32[]{:S(2)}) copy-start(f32[36,32,128]{2,1,0:T(8,128)} %get-tuple-element.506) | copy-start | bytes 1769476 | tf_op jit(solution)/shard_map/while
  78.4 4.1 %copy-start.4 = (f32[36,32,128]{2,1,0:T(8,128)S(1)}, f32[36,32,128]{2,1,0:T(8,128)}, u32[]{:S(2)}) copy-start(f32[36,32,128]{2,1,0:T(8,128)} %get-tuple-element.505) | copy-start | bytes 1769476 | tf_op jit(solution)/shard_map/while
  78.4 4.1 %copy-start.6 = (f32[36,32,128]{2,1,0:T(8,128)S(1)}, f32[36,32,128]{2,1,0:T(8,128)}, u32[]{:S(2)}) copy-start(f32[36,32,128]{2,1,0:T(8,128)} %get-tuple-element.506) | copy-start | bytes 1769476 | tf_op jit(solution)/shard_map/while
  85.8 4.1 %copy-start.4 = (f32[36,32,128]{2,1,0:T(8,128)S(1)}, f32[36,32,128]{2,1,0:T(8,128)}, u32[]{:S(2)}) copy-start(f32[36,32,128]{2,1,0:T(8,128)} %get-tuple-element.505) | copy-start | bytes 1769476 | tf_op jit(solution)/shard_map/while
  85.8 4.1 %copy-start.6 = (f32[36,32,128]{2,1,0:T(8,128)S(1)}, f32[36,32,128]{2,1,0:T(8,128)}, u32[]{:S(2)}) copy-start(f32[36,32,128]{2,1,0:T(8,128)} %get-tuple-element.506) | copy-start | bytes 1769476 | tf_op jit(solution)/shard_map/while
  93.3 4.1 %copy-start.4 = (f32[36,32,128]{2,1,0:T(8,128)S(1)}, f32[36,32,128]{2,1,0:T(8,128)}, u32[]{:S(2)}) copy-start(f32[36,32,128]{2,1,0:T(8,128)} %get-tuple-element.505) | copy-start | bytes 1769476 | tf_op jit(solution)/shard_map/while
  93.3 4.1 %copy-start.6 = (f32[36,32,128]{2,1,0:T(8,128)S(1)}, f32[36,32,128]{2,1,0:T(8,128)}, u32[]{:S(2)}) copy-start(f32[36,32,128]{2,1,0:T(8,128)} %get-tuple-element.506) | copy-start | bytes 1769476 | tf_op jit(solution)/shard_map/while
  100.7 4.1 %copy-start.4 = (f32[36,32,128]{2,1,0:T(8,128)S(1)}, f32[36,32,128]{2,1,0:T(8,128)}, u32[]{:S(2)}) copy-start(f32[36,32,128]{2,1,0:T(8,128)} %get-tuple-element.505) | copy-start | bytes 1769476 | tf_op jit(solution)/shard_map/while
  100.7 4.1 %copy-start.6 = (f32[36,32,128]{2,1,0:T(8,128)S(1)}, f32[36,32,128]{2,1,0:T(8,128)}, u32[]{:S(2)}) copy-start(f32[36,32,128]{2,1,0:T(8,128)} %get-tuple-element.506) | copy-start | bytes 1769476 | tf_op jit(solution)/shard_map/while
  108.8 20.4 %copy-start.13 = (f32[36,64,128]{2,1,0:T(8,128)}, f32[36,64,128]{2,1,0:T(8,128)S(1)}, u32[]{:S(2)}) copy-start(f32[36,64,128]{2,1,0:T(8,128)S(1)} %constant_dynamic-update-slice_fusion.3) | copy-start | bytes 3538948
  108.8 6.6 %collective-permute-start.4 = (f32[1,6,64,128]{3,2,1,0:T(8,128)S(1)}, f32[1,6,64,128]{3,2,1,0:T(8,128)S(1)}, u32[]{:S(2)}, u32[]{:S(2)}) collective-permute-start(f32[1,6,64,128]{3,2,1,0:T(8,128)S(1)} %get-tuple-element.278), channel_id=1, source_target_pairs={{0,8},{8,16},{16,24},{24,0},{1,9},{9,17},{17,25},{25,1},{2,10},{10... | collective-permute-start | bytes 589832 | tf_op jit(solution)/shard_map/ppermute | solution.py:18
  110.4 7.6 %collective-permute-start.5 = (f32[1,6,64,128]{3,2,1,0:T(8,128)S(1)}, f32[1,6,64,128]{3,2,1,0:T(8,128)S(1)}, u32[]{:S(2)}, u32[]{:S(2)}) collective-permute-start(f32[1,6,64,128]{3,2,1,0:T(8,128)S(1)} %get-tuple-element.279), channel_id=1, source_target_pairs={{8,0},{16,8},{24,16},{0,24},{9,1},{17,9},{25,17},{1,25},{10,2},{18... | collective-permute-start | bytes 589832 | tf_op jit(solution)/shard_map/ppermute | solution.py:20
  118.7 9.7 %collective-permute-start.6 = (f32[8,1,64,128]{3,2,1,0:T(8,128)S(1)}, f32[8,1,64,128]{3,2,1,0:T(8,128)S(1)}, u32[]{:S(2)}, u32[]{:S(2)}) collective-permute-start(f32[8,1,64,128]{3,2,1,0:T(8,128)S(1)} %get-tuple-element.270), channel_id=1, source_target_pairs={{0,1},{1,2},{2,3},{3,4},{4,5},{5,6},{6,7},{7,0},{8,9},{9,10},{10,1... | collective-permute-start | bytes 786440 | tf_op jit(solution)/shard_map/ppermute | solution.py:18
  118.8 10.3 %collective-permute-start.7 = (f32[8,1,64,128]{3,2,1,0:T(8,128)S(1)}, f32[8,1,64,128]{3,2,1,0:T(8,128)}, u32[]{:S(2)}, u32[]{:S(2)}) collective-permute-start(f32[8,1,64,128]{3,2,1,0:T(8,128)S(1)} %get-tuple-element.271), channel_id=1, source_target_pairs={{1,0},{2,1},{3,2},{4,3},{5,4},{6,5},{7,6},{0,7},{9,8},{10,9},{11,1... | collective-permute-start | bytes 786440 | tf_op jit(solution)/shard_map/ppermute | solution.py:20
  133.6 4.1 %copy-start.9 = (f32[36,32,128]{2,1,0:T(8,128)S(1)}, f32[36,32,128]{2,1,0:T(8,128)}, u32[]{:S(2)}) copy-start(f32[36,32,128]{2,1,0:T(8,128)} %get-tuple-element.541) | copy-start | bytes 1769476 | tf_op jit(solution)/shard_map/while
  133.6 4.1 %copy-start.11 = (f32[36,32,128]{2,1,0:T(8,128)S(1)}, f32[36,32,128]{2,1,0:T(8,128)}, u32[]{:S(2)}) copy-start(f32[36,32,128]{2,1,0:T(8,128)} %get-tuple-element.542) | copy-start | bytes 1769476 | tf_op jit(solution)/shard_map/while
  141.0 4.1 %copy-start.9 = (f32[36,32,128]{2,1,0:T(8,128)S(1)}, f32[36,32,128]{2,1,0:T(8,128)}, u32[]{:S(2)}) copy-start(f32[36,32,128]{2,1,0:T(8,128)} %get-tuple-element.541) | copy-start | bytes 1769476 | tf_op jit(solution)/shard_map/while
  141.0 4.1 %copy-start.11 = (f32[36,32,128]{2,1,0:T(8,128)S(1)}, f32[36,32,128]{2,1,0:T(8,128)}, u32[]{:S(2)}) copy-start(f32[36,32,128]{2,1,0:T(8,128)} %get-tuple-element.542) | copy-start | bytes 1769476 | tf_op jit(solution)/shard_map/while
  148.4 4.1 %copy-start.9 = (f32[36,32,128]{2,1,0:T(8,128)S(1)}, f32[36,32,128]{2,1,0:T(8,128)}, u32[]{:S(2)}) copy-start(f32[36,32,128]{2,1,0:T(8,128)} %get-tuple-element.541) | copy-start | bytes 1769476 | tf_op jit(solution)/shard_map/while
  148.4 4.1 %copy-start.11 = (f32[36,32,128]{2,1,0:T(8,128)S(1)}, f32[36,32,128]{2,1,0:T(8,128)}, u32[]{:S(2)}) copy-start(f32[36,32,128]{2,1,0:T(8,128)} %get-tuple-element.542) | copy-start | bytes 1769476 | tf_op jit(solution)/shard_map/while
  155.9 4.1 %copy-start.9 = (f32[36,32,128]{2,1,0:T(8,128)S(1)}, f32[36,32,128]{2,1,0:T(8,128)}, u32[]{:S(2)}) copy-start(f32[36,32,128]{2,1,0:T(8,128)} %get-tuple-element.541) | copy-start | bytes 1769476 | tf_op jit(solution)/shard_map/while
  155.9 4.1 %copy-start.11 = (f32[36,32,128]{2,1,0:T(8,128)S(1)}, f32[36,32,128]{2,1,0:T(8,128)}, u32[]{:S(2)}) copy-start(f32[36,32,128]{2,1,0:T(8,128)} %get-tuple-element.542) | copy-start | bytes 1769476 | tf_op jit(solution)/shard_map/while
  163.3 4.1 %copy-start.9 = (f32[36,32,128]{2,1,0:T(8,128)S(1)}, f32[36,32,128]{2,1,0:T(8,128)}, u32[]{:S(2)}) copy-start(f32[36,32,128]{2,1,0:T(8,128)} %get-tuple-element.541) | copy-start | bytes 1769476 | tf_op jit(solution)/shard_map/while
  163.3 4.1 %copy-start.11 = (f32[36,32,128]{2,1,0:T(8,128)S(1)}, f32[36,32,128]{2,1,0:T(8,128)}, u32[]{:S(2)}) copy-start(f32[36,32,128]{2,1,0:T(8,128)} %get-tuple-element.542) | copy-start | bytes 1769476 | tf_op jit(solution)/shard_map/while
  170.7 4.1 %copy-start.9 = (f32[36,32,128]{2,1,0:T(8,128)S(1)}, f32[36,32,128]{2,1,0:T(8,128)}, u32[]{:S(2)}) copy-start(f32[36,32,128]{2,1,0:T(8,128)} %get-tuple-element.541) | copy-start | bytes 1769476 | tf_op jit(solution)/shard_map/while
  170.8 4.1 %copy-start.11 = (f32[36,32,128]{2,1,0:T(8,128)S(1)}, f32[36,32,128]{2,1,0:T(8,128)}, u32[]{:S(2)}) copy-start(f32[36,32,128]{2,1,0:T(8,128)} %get-tuple-element.542) | copy-start | bytes 1769476 | tf_op jit(solution)/shard_map/while
  178.2 4.1 %copy-start.9 = (f32[36,32,128]{2,1,0:T(8,128)S(1)}, f32[36,32,128]{2,1,0:T(8,128)}, u32[]{:S(2)}) copy-start(f32[36,32,128]{2,1,0:T(8,128)} %get-tuple-element.541) | copy-start | bytes 1769476 | tf_op jit(solution)/shard_map/while
  178.2 4.1 %copy-start.11 = (f32[36,32,128]{2,1,0:T(8,128)S(1)}, f32[36,32,128]{2,1,0:T(8,128)}, u32[]{:S(2)}) copy-start(f32[36,32,128]{2,1,0:T(8,128)} %get-tuple-element.542) | copy-start | bytes 1769476 | tf_op jit(solution)/shard_map/while
  185.6 4.1 %copy-start.9 = (f32[36,32,128]{2,1,0:T(8,128)S(1)}, f32[36,32,128]{2,1,0:T(8,128)}, u32[]{:S(2)}) copy-start(f32[36,32,128]{2,1,0:T(8,128)} %get-tuple-element.541) | copy-start | bytes 1769476 | tf_op jit(solution)/shard_map/while
  185.6 4.1 %copy-start.11 = (f32[36,32,128]{2,1,0:T(8,128)S(1)}, f32[36,32,128]{2,1,0:T(8,128)}, u32[]{:S(2)}) copy-start(f32[36,32,128]{2,1,0:T(8,128)} %get-tuple-element.542) | copy-start | bytes 1769476 | tf_op jit(solution)/shard_map/while
  193.1 4.1 %copy-start.9 = (f32[36,32,128]{2,1,0:T(8,128)S(1)}, f32[36,32,128]{2,1,0:T(8,128)}, u32[]{:S(2)}) copy-start(f32[36,32,128]{2,1,0:T(8,128)} %get-tuple-element.541) | copy-start | bytes 1769476 | tf_op jit(solution)/shard_map/while
  193.1 4.1 %copy-start.11 = (f32[36,32,128]{2,1,0:T(8,128)S(1)}, f32[36,32,128]{2,1,0:T(8,128)}, u32[]{:S(2)}) copy-start(f32[36,32,128]{2,1,0:T(8,128)} %get-tuple-element.542) | copy-start | bytes 1769476 | tf_op jit(solution)/shard_map/while
  201.6 21.4 %copy-start.15 = (f32[6,6,64,128]{3,2,1,0:T(8,128)}, f32[6,6,64,128]{3,2,1,0:T(8,128)S(1)}, u32[]{:S(2)}) copy-start(f32[6,6,64,128]{3,2,1,0:T(8,128)S(1)} %sub.47) | copy-start | bytes 3538948
  201.7 6.6 %collective-permute-start.8 = (f32[1,6,64,128]{3,2,1,0:T(8,128)S(1)}, f32[1,6,64,128]{3,2,1,0:T(8,128)S(1)}, u32[]{:S(2)}, u32[]{:S(2)}) collective-permute-start(f32[1,6,64,128]{3,2,1,0:T(8,128)S(1)} %get-tuple-element.276), channel_id=1, source_target_pairs={{0,8},{8,16},{16,24},{24,0},{1,9},{9,17},{17,25},{25,1},{2,10},{10... | collective-permute-start | bytes 589832 | tf_op jit(solution)/shard_map/ppermute | solution.py:18
  201.7 10.7 %collective-permute-start.9 = (f32[1,6,64,128]{3,2,1,0:T(8,128)S(1)}, f32[1,6,64,128]{3,2,1,0:T(8,128)S(1)}, u32[]{:S(2)}, u32[]{:S(2)}) collective-permute-start(f32[1,6,64,128]{3,2,1,0:T(8,128)S(1)} %get-tuple-element.277), channel_id=1, source_target_pairs={{8,0},{16,8},{24,16},{0,24},{9,1},{17,9},{25,17},{1,25},{10,2},{18... | collective-permute-start | bytes 589832 | tf_op jit(solution)/shard_map/ppermute | solution.py:20
  213.1 9.2 %collective-permute-start.10 = (f32[8,1,64,128]{3,2,1,0:T(8,128)S(1)}, f32[8,1,64,128]{3,2,1,0:T(8,128)S(1)}, u32[]{:S(2)}, u32[]{:S(2)}) collective-permute-start(f32[8,1,64,128]{3,2,1,0:T(8,128)S(1)} %get-tuple-element.268), channel_id=1, source_target_pairs={{0,1},{1,2},{2,3},{3,4},{4,5},{5,6},{6,7},{7,0},{8,9},{9,10},{10,1... | collective-permute-start | bytes 786440 | tf_op jit(solution)/shard_map/ppermute | solution.py:18
  213.2 9.8 %collective-permute-start.11 = (f32[8,1,64,128]{3,2,1,0:T(8,128)S(1)}, f32[8,1,64,128]{3,2,1,0:T(8,128)}, u32[]{:S(2)}, u32[]{:S(2)}) collective-permute-start(f32[8,1,64,128]{3,2,1,0:T(8,128)S(1)} %get-tuple-element.269), channel_id=1, source_target_pairs={{1,0},{2,1},{3,2},{4,3},{5,4},{6,5},{7,6},{0,7},{9,8},{10,9},{11,1... | collective-permute-start | bytes 786440 | tf_op jit(solution)/shard_map/ppermute | solution.py:20
  227.7 4.1 %copy-start = (f32[36,32,128]{2,1,0:T(8,128)S(1)}, f32[36,32,128]{2,1,0:T(8,128)}, u32[]{:S(2)}) copy-start(f32[36,32,128]{2,1,0:T(8,128)} %get-tuple-element.577) | copy-start | bytes 1769476 | tf_op jit(solution)/shard_map/while
  227.7 4.1 %copy-start.2 = (f32[36,32,128]{2,1,0:T(8,128)S(1)}, f32[36,32,128]{2,1,0:T(8,128)}, u32[]{:S(2)}) copy-start(f32[36,32,128]{2,1,0:T(8,128)} %get-tuple-element.578) | copy-start | bytes 1769476 | tf_op jit(solution)/shard_map/while
  235.2 4.1 %copy-start = (f32[36,32,128]{2,1,0:T(8,128)S(1)}, f32[36,32,128]{2,1,0:T(8,128)}, u32[]{:S(2)}) copy-start(f32[36,32,128]{2,1,0:T(8,128)} %get-tuple-element.577) | copy-start | bytes 1769476 | tf_op jit(solution)/shard_map/while
  250.1 4.1 %copy-start = (f32[36,32,128]{2,1,0:T(8,128)S(1)}, f32[36,32,128]{2,1,0:T(8,128)}, u32[]{:S(2)}) copy-start(f32[36,32,128]{2,1,0:T(8,128)} %get-tuple-element.577) | copy-start | bytes 1769476 | tf_op jit(solution)/shard_map/while
  250.2 4.1 %copy-start.2 = (f32[36,32,128]{2,1,0:T(8,128)S(1)}, f32[36,32,128]{2,1,0:T(8,128)}, u32[]{:S(2)}) copy-start(f32[36,32,128]{2,1,0:T(8,128)} %get-tuple-element.578) | copy-start | bytes 1769476 | tf_op jit(solution)/shard_map/while
  257.6 4.1 %copy-start = (f32[36,32,128]{2,1,0:T(8,128)S(1)}, f32[36,32,128]{2,1,0:T(8,128)}, u32[]{:S(2)}) copy-start(f32[36,32,128]{2,1,0:T(8,128)} %get-tuple-element.577) | copy-start | bytes 1769476 | tf_op jit(solution)/shard_map/while
  257.6 4.1 %copy-start.2 = (f32[36,32,128]{2,1,0:T(8,128)S(1)}, f32[36,32,128]{2,1,0:T(8,128)}, u32[]{:S(2)}) copy-start(f32[36,32,128]{2,1,0:T(8,128)} %get-tuple-element.578) | copy-start | bytes 1769476 | tf_op jit(solution)/shard_map/while
  265.1 4.1 %copy-start = (f32[36,32,128]{2,1,0:T(8,128)S(1)}, f32[36,32,128]{2,1,0:T(8,128)}, u32[]{:S(2)}) copy-start(f32[36,32,128]{2,1,0:T(8,128)} %get-tuple-element.577) | copy-start | bytes 1769476 | tf_op jit(solution)/shard_map/while
  265.1 4.1 %copy-start.2 = (f32[36,32,128]{2,1,0:T(8,128)S(1)}, f32[36,32,128]{2,1,0:T(8,128)}, u32[]{:S(2)}) copy-start(f32[36,32,128]{2,1,0:T(8,128)} %get-tuple-element.578) | copy-start | bytes 1769476 | tf_op jit(solution)/shard_map/while
  272.6 4.1 %copy-start = (f32[36,32,128]{2,1,0:T(8,128)S(1)}, f32[36,32,128]{2,1,0:T(8,128)}, u32[]{:S(2)}) copy-start(f32[36,32,128]{2,1,0:T(8,128)} %get-tuple-element.577) | copy-start | bytes 1769476 | tf_op jit(solution)/shard_map/while
  272.6 4.1 %copy-start.2 = (f32[36,32,128]{2,1,0:T(8,128)S(1)}, f32[36,32,128]{2,1,0:T(8,128)}, u32[]{:S(2)}) copy-start(f32[36,32,128]{2,1,0:T(8,128)} %get-tuple-element.578) | copy-start | bytes 1769476 | tf_op jit(solution)/shard_map/while
  (72 other events, 85.5 us)
where the time goes:
time: 338 us; the launch traced here: 336 us
  matrix products  108 us (32%)
  local copies, waits for them, and re-layouts  93.3 us (28%)
  blocking collectives  36.9 us (11%)
  waiting for transfers between devices  29.9 us (9%)
  other arithmetic  24.5 us (7%)
  loops' own time  21.9 us (6%)
  starting transfers between devices  20.8 us (6%)
    dot_general x27, matrix products, accumulate(): jnp.einsum('npb,nba->npa', piece, chosen, precision=lax.Precision.HIGHEST)  108 us
    while x216, local copies, waits for them, and re-layouts  44.5 us
    psum x1, blocking collectives, reduce_one(): return lax.psum(intersection(probes, field), ('gx', 'gy')) * scale  36.9 us
    unnamed x36, local copies, waits for them, and re-layouts  22.6 us
    another operation x3, loops' own time, apply_hamiltonian(): lax.fori_loop(0, slot_bound, accumulate, (zeros, zeros))  21.9 us
    ppermute x6, waiting for transfers between devices, with_halo(): lax.ppermute(tail, axis, [(i, (i + 1) % count) for i in range(count)])  19.8 us
    gather x27, local copies, waits for them, and re-layouts, accumulate(): piece = jnp.take(source, flat_partner[:, slot], axis=0)  16.9 us
    ppermute x6, starting transfers between devices, with_halo(): lax.ppermute(head, axis, [((i + 1) % count, i) for i in range(count)])  16 us
  transfers between devices with their start and end apart: 12, of which 8 were waited for; matrix products, arithmetic and copies ran while one was open for 6% of the time, Pallas kernels for 0%

commit v1 on v0

v1 whole, which is shorter than its diff:
```python
import functools
import math

import jax
import jax.numpy as jnp
from jax import lax
from jax.experimental import pallas as pl
from jax.experimental.pallas import tpu as pltpu
from jax.sharding import PartitionSpec as P

STEPS = 3
MESH = pl.DeviceIdType.MESH
F32, BF16 = jnp.float32, jnp.bfloat16


def kernel(
    axes, table, counts, phase, v0_hbm, blocks_hbm, last, total,
    v0, v1, v2, halo_x, halo_y, field_a, field_b, landed, weights, sums, ring_x, ring_y,
    v0_sem, land_sem, send_sem, recv_sem, sum_send_x, sum_recv_x, sum_send_y, sum_recv_y,
):
    (name_x, size_x), (name_y, size_y) = axes
    cx, cy, width, block = v0.shape
    slots = landed.shape[1]
    half = width // 2
    pitch = cy + 2
    me_x, me_y = lax.axis_index(name_x), lax.axis_index(name_y)
    vectors = (v0, v1, v2, last)
    fields = (field_a, field_b)

    def landing(x, y):
        i = x * cy + y
        return pltpu.make_async_copy(blocks_hbm.at[x, y], landed.at[i], land_sem.at[i])

    def interior(k):
        return 1 + k // (cy - 2), 1 + k % (cy - 2)

    def rim_y(k):
        return 1 + k // 2, (k % 2) * (cy - 1)

    def rim_x(k):
        return (k // (cy - 2)) * (cx - 1), 1 + k % (cy - 2)

    def corner(k):
        return (k // 2) * (cx - 1), (k % 2) * (cy - 1)

    groups = (
        (interior, (cx - 2) * (cy - 2)),
        (rim_y, 2 * (cx - 2)),
        (rim_x, 2 * (cy - 2)),
        (corner, 4),
    )

    load_v0 = pltpu.make_async_copy(v0_hbm, v0, v0_sem)
    load_v0.start()
    for place, count in groups:

        @pl.loop(0, count)
        def _(k):
            landing(*place(k)).start()

    barrier = pltpu.get_barrier_semaphore()
    for name, size, me in ((name_x, size_x, me_x), (name_y, size_y, me_y)):
        for j in range(1, size):
            pl.semaphore_signal(
                barrier, inc=1, device_id={name: lax.rem(me + j, size)}, device_id_type=MESH
            )
    pl.semaphore_wait(barrier, size_x + size_y - 2)

    def towards(name, size, me, side):
        return {name: lax.rem(me + (size - 1 if side else 1), size)}

    def remote(step, kind, src, dst, peer):
        return pltpu.make_async_remote_copy(
            src_ref=src,
            dst_ref=dst,
            send_sem=send_sem.at[step, kind],
            recv_sem=recv_sem.at[step, kind],
            device_id=peer,
            device_id_type=MESH,
        )

    def x_copies(step, part):
        first, length = ((1, cy - 2), (0, 1), (cy - 1, 1))[part]
        return [
            remote(
                step,
                2 * part + side,
                vectors[step].at[0 if side else cx - 1, pl.ds(first, length)],
                halo_x.at[step, side, pl.ds(first, length)],
                towards(name_x, size_x, me_x, side),
            )
            for side in range(2)
        ]

    def y_copies(step):
        return [
            remote(
                step,
                6 + side,
                vectors[step].at[:, 0 if side else cy - 1],
                halo_y.at[step, side, pl.ds(1, cx)],
                towards(name_y, size_y, me_y, side),
            )
            for side in range(2)
        ]

    def corner_copies(step):
        return [
            remote(
                step,
                8 + 2 * side + end,
                halo_x.at[step, end, 0 if side else cy - 1],
                halo_y.at[step, side, end * (cx + 1)],
                towards(name_y, size_y, me_y, side),
            )
            for side in range(2)
            for end in range(2)
        ]

    def start(copies):
        for copy in copies:
            copy.start()

    def arrive(copies):
        for copy in copies:
            copy.wait_recv()

    def put(field, position, value):
        high = value.astype(BF16)
        field[position, :width] = high
        field[position, width:] = (value - high.astype(F32)).astype(BF16)

    def put_turned(field, position, value, at_x, at_y):
        entry = at_x * 3 + at_y
        cosine, sine = phase[entry], phase[9 + entry]
        real, imag = value[:half], value[half:]
        put(
            field,
            position,
            jnp.concatenate(
                [cosine * real - sine * imag, sine * real + cosine * imag], axis=0
            ),
        )

    def prepare(x, y):
        i = x * cy + y
        landing(x, y).wait()
        count = counts[i]
        for s in range(slots):
            entry = landed[i, s] * jnp.where(s < count, 1.0, 0.0).astype(F32)
            high = entry.astype(BF16)
            weights[i, s * block : (s + 1) * block, :block] = high
            weights[i, s * block : (s + 1) * block, block:] = (
                entry - high.astype(F32)
            ).astype(BF16)

    def advance(step, x, y):
        i = x * cy + y
        source = fields[step % 2]
        lhs = jnp.concatenate([source[table[i * slots + s]] for s in range(slots)], axis=1)
        product = jnp.dot(lhs, weights[i], preferred_element_type=F32)
        value = product[:width, :block] + (
            product[width:, :block] + product[:width, block:] + product[width:, block:]
        )
        if step:
            value = 2.0 * value - vectors[step - 1][x, y]
        vectors[step + 1][x, y] = value
        if step + 1 < STEPS:
            put(fields[(step + 1) % 2], (x + 1) * pitch + y + 1, value)
        start_vector = v0[x, y]
        first_re, first_im = start_vector[:half], start_vector[half:]
        other_re, other_im = value[:half], value[half:]
        low = step * width
        sums[low : low + half] += first_re * other_re + first_im * other_im
        sums[low + half : low + width] += first_re * other_im - first_im * other_re

    def run(step, group):
        place, count = groups[group]

        def body(k, carry):
            x, y = place(k)
            if step == 0:
                prepare(x, y)
            advance(step, x, y)
            return carry

        lax.fori_loop(0, count, body, 0, unroll=1 if step == 0 else 2)

    load_v0.wait()
    start(x_copies(0, 1) + x_copies(0, 2) + y_copies(0) + x_copies(0, 0))
    sums[...] = jnp.zeros_like(sums)

    @pl.loop(0, cx * cy)
    def _(k):
        x, y = k // cy, k % cy
        put(field_a, (x + 1) * pitch + y + 1, v0[x, y])

    for step in range(STEPS):
        field = fields[step % 2]
        run(step, 0)
        arrive(y_copies(step))
        for side in range(2):

            @pl.loop(0, cx)
            def _(x):
                put_turned(
                    field,
                    (x + 1) * pitch + side * (cy + 1),
                    halo_y[step, side, x + 1],
                    1,
                    2 * side,
                )

        run(step, 1)
        arrive(x_copies(step, 1) + x_copies(step, 2))
        start(corner_copies(step))
        arrive(x_copies(step, 0))
        for side in range(2):

            @pl.loop(0, cy)
            def _(y):
                put_turned(
                    field,
                    side * (cx + 1) * pitch + y + 1,
                    halo_x[step, side, y],
                    2 * side,
                    1,
                )

        run(step, 2)
        if step + 1 < STEPS:
            start(x_copies(step + 1, 0))
        arrive(corner_copies(step))
        for side in range(2):
            for end in range(2):
                put_turned(
                    field,
                    end * (cx + 1) * pitch + side * (cy + 1),
                    halo_y[step, side, end * (cx + 1)],
                    2 * end,
                    2 * side,
                )
        run(step, 3)
        if step + 1 < STEPS:
            start(x_copies(step + 1, 1) + x_copies(step + 1, 2) + y_copies(step + 1))

    found = lax.dot_general(
        jnp.ones((8, block), F32),
        sums[...],
        (((1,), (1,)), ((), ())),
        precision=lax.Precision.HIGHEST,
        preferred_element_type=F32,
    )
    for name, size, me, ring, sent, got in (
        (name_x, size_x, me_x, ring_x, sum_send_x, sum_recv_x),
        (name_y, size_y, me_y, ring_y, sum_send_y, sum_recv_y),
    ):
        ring[me] = found
        copies = [
            pltpu.make_async_remote_copy(
                src_ref=ring.at[me],
                dst_ref=ring.at[me],
                send_sem=sent.at[j],
                recv_sem=got.at[j],
                device_id={name: lax.rem(me + j, size)},
                device_id_type=MESH,
            )
            for j in range(1, size)
        ]
        start(copies)
        for copy in copies:
            copy.wait()
        found = ring[0]
        for j in range(1, size):
            found = found + ring[j]
    total[...] = found
    for step in range(STEPS):
        for copy in (
            x_copies(step, 0) + x_copies(step, 1) + x_copies(step, 2)
            + y_copies(step) + corner_copies(step)
        ):
            copy.wait_send()


def shards(axes, probes, pair_blocks, partners, shifts, counts, kpoint):
    (name_x, size_x), (name_y, size_y) = axes
    cx, cy, width, block = probes.shape
    slots = pair_blocks.shape[2]
    cells = cx * cy
    total_x, total_y = cx * size_x, cy * size_y
    me_x, me_y = lax.axis_index(name_x), lax.axis_index(name_y)
    at_x = jnp.mod(partners // total_y - me_x * cx + 1, total_x)
    at_y = jnp.mod(partners % total_y - me_y * cy + 1, total_y)
    table = (at_x * (cy + 2) + at_y).reshape(cells * slots)
    side = jnp.arange(3, dtype=jnp.int32)

    def crossing(me, size):
        return jnp.where(
            (side == 0) & (me == 0), -1, jnp.where((side == 2) & (me == size - 1), 1, 0)
        ).astype(F32)

    angle = (
        kpoint[0] * crossing(me_x, size_x)[:, None] + kpoint[1] * crossing(me_y, size_y)[None, :]
    ).reshape(9)
    phase = jnp.concatenate([jnp.cos(angle), jnp.sin(angle)])
    rows = STEPS * width
    halo = (width, block)
    smem = pl.BlockSpec(memory_space=pltpu.SMEM)
    anywhere = pl.BlockSpec(memory_space=pl.ANY)
    vmem = pl.BlockSpec(memory_space=pltpu.VMEM)
    dma = pltpu.SemaphoreType.DMA
    last, found = pl.pallas_call(
        functools.partial(kernel, axes),
        out_shape=(
            jax.ShapeDtypeStruct(probes.shape, F32),
            jax.ShapeDtypeStruct((8, rows), F32),
        ),
        in_specs=[smem, smem, smem, anywhere, anywhere],
        out_specs=(vmem, vmem),
        scratch_shapes=[
            pltpu.VMEM(probes.shape, F32),
            pltpu.VMEM(probes.shape, F32),
            pltpu.VMEM(probes.shape, F32),
            pltpu.VMEM((STEPS, 2, cy) + halo, F32),
            pltpu.VMEM((STEPS, 2, cx + 2) + halo, F32),
            pltpu.VMEM(((cx + 2) * (cy + 2), 2 * width, block), BF16),
            pltpu.VMEM(((cx + 2) * (cy + 2), 2 * width, block), BF16),
            pltpu.VMEM((cells, slots, block, block), F32),
            pltpu.VMEM((cells, slots * block, 2 * block), BF16),
            pltpu.VMEM((rows, block), F32),
            pltpu.VMEM((size_x, 8, rows), F32),
            pltpu.VMEM((size_y, 8, rows), F32),
            dma(()),
            dma((cells,)),
            dma((STEPS, 12)),
            dma((STEPS, 12)),
            dma((size_x,)),
            dma((size_x,)),
            dma((size_y,)),
            dma((size_y,)),
        ],
        compiler_params=pltpu.CompilerParams(
            collective_id=0, has_side_effects=True, vmem_limit_bytes=66_000_000
        ),
    )(table, counts.reshape(cells), phase, probes, pair_blocks)
    scale = 1.0 / math.sqrt(total_x * total_y * block)
    return last, (found[0] * scale).reshape(STEPS, 2, width // 2)


def solution(mesh):
    placed = (
        P("gx", "gy", None, None),
        P("gx", "gy", None, None, None),
        P("gx", "gy", None),
        P(None, "gx", "gy", None),
        P("gx", "gy"),
        P(),
    )
    axes = tuple((name, mesh.shape[name]) for name in ("gx", "gy"))
    return jax.shard_map(
        functools.partial(shards, axes),
        mesh=mesh,
        in_specs=placed,
        out_specs=(P("gx", "gy", None, None), P()),
        check_vma=False,
    )
```

time: 338 us -> 66.4 us (0.20)
  matrix products: 108 us -> 0 us
  local copies, waits for them, and re-layouts: 93.3 us -> 6.54 us
  Pallas kernels: 0 us -> 55.4 us
  blocking collectives: 36.9 us -> 0 us
  waiting for transfers between devices: 29.9 us -> 0 us
  loops' own time: 21.9 us -> 0 us
  other arithmetic: 24.5 us -> 3.53 us
  starting transfers between devices: 20.8 us -> 0 us
    dot_general x27 -> x0, matrix products: 108 us -> none  [accumulate(): jnp.einsum('npb,nba->npa', piece, chosen, precision=lax.Precision.HIGHEST)]
    pallas_call x0 -> x1, Pallas kernels: none -> 55.4 us  [shards(): pl.pallas_call(functools.partial(kernel, axes), out_shape=(jax.ShapeDtype...]
    while x219 -> x0, local copies, waits for them, and re-layouts: 44.8 us -> none
    psum x1 -> x0, blocking collectives: 36.9 us -> none  [reduce_one(): return lax.psum(intersection(probes, field), ('gx', 'gy')) * scale]
    ppermute x12 -> x0, waiting for transfers between devices: 29.9 us -> none  [the longest x6 19.8 us: with_halo(): lax.ppermute(tail, axis, [(i, (i + 1) % count) for i in range(count)])]
    another operation x3 -> x0, loops' own time: 21.9 us -> none  [apply_hamiltonian(): lax.fori_loop(0, slot_bound, accumulate, (zeros, zeros))]
    ppermute x12 -> x0, starting transfers between devices: 20.8 us -> none  [the longest x6 16 us: with_halo(): lax.ppermute(head, axis, [((i + 1) % count, i) for i in range(count)])]
    unnamed x36 -> x1, local copies, waits for them, and re-layouts: 22.6 us -> 2.41 us
  transfers between devices with their start and end apart: 12 -> 0, of which waited for: 8 -> 0; matrix products, arithmetic and copies ran while one was open for 6% -> 0% of each run, Pallas kernels for 0% -> 0%
where the time goes in v1:
time: 66.4 us; the launch traced here: 66.1 us
  Pallas kernels  55.4 us (83%)
  local copies, waits for them, and re-layouts  6.54 us (10%)
  other arithmetic  3.53 us (5%)
    pallas_call x1, Pallas kernels, shards(): pl.pallas_call(functools.partial(kernel, axes), out_shape=(jax.ShapeDtype...  55.4 us
    unnamed x1, local copies, waits for them, and re-layouts  2.41 us
    slice x1, local copies, waits for them, and re-layouts, shards(): kpoint[0] * crossing(me_x, size_x)[:, None]  1.34 us

profile of v1, /device:TPU:0, one launch (start us, length us, event | category | flops | bytes accessed | tf_op | source)
XLA Modules:
  0.0 66.1 jit_solution(10980573655097676335)
XLA Ops:
  0.6 1.3 %reshape.47.counts = s32[36]{0:T(128)} reshape(s32[6,6]{1,0:T(8,128)} %param.9) | data formatting | bytes 288 | tf_op jit(solution)/shard_map/reshape | solution.py:345
  1.9 1.3 %fusion.9 = (f32[1]{0:T(128)}, f32[1]{0:T(128)}) fusion(f32[2]{0:T(128)} %param.10), kind=kLoop, calls=%fused_computation.24 | loop fusion | bytes 16 | tf_op jit(solution)/shard_map/slice | solution.py:303
  3.3 1.3 %convert_multiply_fusion = (f32[3]{0:T(128)S(1)}, f32[3]{0:T(128)S(1)}) fusion(pred[]{:T(512)S(6)} %eq.49, pred[]{:T(512)S(6)} %eq.48, f32[]{:T(128)} %bitcast.1, pred[]{:T(512)S(6)} %eq.47, pred[]{:T(512)S(6)} %eq.45, f32[]{:T(128)} %bitcast), kind=kLoop, calls=%fused_computation.22 | loop fusion | flops 42 | bytes 36 | tf_op jit(solution)/shard_map/mul | solution.py:303
  4.6 0.1 add_cosine_fusion
  4.7 0.1 cos.7
  4.7 0.1 sin.7
  4.8 0.6 pad_maximum_fusion.phase
  5.4 0.8 %fusion.4 = s32[6,6,9]{2,1,0:T(8,128)S(1)} fusion(s32[6,6,9]{2,1,0:T(8,128)} %param.8, s32[]{:T(128)S(6)} %mul.47, s32[]{:T(128)S(6)} %mul.44), kind=kLoop, calls=%fused_computation.8 | loop fusion | flops 9720 | bytes 2600 | tf_op jit(solution)/shard_map/add | solution.py:294
  6.2 0.7 %reshape.46.table = s32[324]{0:T(512)} reshape(s32[6,6,9]{2,1,0:T(8,128)S(1)} %fusion.4) | data formatting | bytes 2592 | tf_op jit(solution)/shard_map/reshape | solution.py:294
  6.9 55.4 %shard_map.68 = (f32[6,6,64,128]{3,2,1,0:T(8,128)}, f32[8,192]{1,0:T(8,128)}) custom-call(s32[324]{0:T(512)} %reshape.46.table, s32[36]{0:T(128)} %reshape.47.counts, f32[18]{0:T(128)} %pad_maximum_fusion.phase, f32[6,6,64,128]{3,2,1,0:T(8,128)} %v0_hbm.1, f32[6,6,9,128,128]{4,3,2,1,0:T(8,128)} %blocks_hbm.1), custom_call_target="tpu_custom_call" | custom-call | tf_op jit(solution)/shard_map/pallas_call | solution.py:312
  62.3 0.7 %multiply_reduce_fusion = f32[192]{0:T(256)S(1)} fusion(f32[8,192]{1,0:T(8,128)} %get-tuple-element.5), kind=kLoop, calls=%fused_computation.20 | loop fusion | flops 192 | bytes 1536 | tf_op jit(solution)/shard_map/mul | solution.py:347
  63.0 0.7 %mul.54 = f32[3,2,32]{2,1,0:T(2,128)} reshape(f32[192]{0:T(256)S(1)} %multiply_reduce_fusion) | data formatting | bytes 1536 | tf_op jit(solution)/shard_map/mul | solution.py:347
  63.7 2.4 %copy.8 = f32[6,6,64,128]{3,2,1,0:T(8,128)} copy(f32[6,6,64,128]{3,2,1,0:T(8,128)} %get-tuple-element.14) | data formatting | bytes 2359296

commit v2 on v1

--- a/solution.py
+++ b/solution.py
@@ -14,8 +14,8 @@
 
 
 def kernel(
-    axes, table, counts, phase, v0_hbm, blocks_hbm, last, total,
-    v0, v1, v2, halo_x, halo_y, field_a, field_b, landed, weights, sums, ring_x, ring_y,
+    axes, partners, counts, kpoint, v0_hbm, blocks_hbm, last, total,
+    v0, v1, v2, halo_x, halo_y, field_a, field_b, landed, weights, sums, ring_x, ring_y, table, turns,
     v0_sem, land_sem, send_sem, recv_sem, sum_send_x, sum_recv_x, sum_send_y, sum_recv_y,
 ):
     (name_x, size_x), (name_y, size_y) = axes
@@ -24,6 +24,7 @@
     half = width // 2
     pitch = cy + 2
     me_x, me_y = lax.axis_index(name_x), lax.axis_index(name_y)
+    total_x, total_y = cx * size_x, cy * size_y
     vectors = (v0, v1, v2, last)
     fields = (field_a, field_b)
 
@@ -31,24 +32,33 @@
         i = x * cy + y
         return pltpu.make_async_copy(blocks_hbm.at[x, y], landed.at[i], land_sem.at[i])
 
+    inner = (cx - 2) * (cy - 2)
+    early = inner // 2
+
     def interior(k):
         return 1 + k // (cy - 2), 1 + k % (cy - 2)
 
     def rim_y(k):
         return 1 + k // 2, (k % 2) * (cy - 1)
 
-    def rim_x(k):
-        return (k // (cy - 2)) * (cx - 1), 1 + k % (cy - 2)
-
     def corner(k):
         return (k // 2) * (cx - 1), (k % 2) * (cy - 1)
 
+    def rim_x_near(k):
+        return (k // 2) * (cx - 1), 1 + (k % 2) * (cy - 3)
+
+    def rim_x_middle(k):
+        return (k // (cy - 4)) * (cx - 1), 2 + k % (cy - 4)
+
     groups = (
-        (interior, (cx - 2) * (cy - 2)),
+        (interior, early),
         (rim_y, 2 * (cx - 2)),
-        (rim_x, 2 * (cy - 2)),
         (corner, 4),
+        (rim_x_near, 4),
+        (rim_x_middle, 2 * (cy - 4)),
+        (lambda k: interior(k + early), inner - early),
     )
+    ends, near, middle = ((0, 1), (cy - 1, 1)), ((1, 1), (cy - 2, 1)), ((2, cy - 4),)
 
     load_v0 = pltpu.make_async_copy(v0_hbm, v0, v0_sem)
     load_v0.start()
@@ -79,16 +89,16 @@
             device_id_type=MESH,
         )
 
-    def x_copies(step, part):
-        first, length = ((1, cy - 2), (0, 1), (cy - 1, 1))[part]
+    def x_copies(step, parts):
         return [
             remote(
                 step,
-                2 * part + side,
+                2 * (ends + near + middle).index((first, length)) + side,
                 vectors[step].at[0 if side else cx - 1, pl.ds(first, length)],
                 halo_x.at[step, side, pl.ds(first, length)],
                 towards(name_x, size_x, me_x, side),
             )
+            for first, length in parts
             for side in range(2)
         ]
 
@@ -96,7 +106,7 @@
         return [
             remote(
                 step,
-                6 + side,
+                10 + side,
                 vectors[step].at[:, 0 if side else cy - 1],
                 halo_y.at[step, side, pl.ds(1, cx)],
                 towards(name_y, size_y, me_y, side),
@@ -108,7 +118,7 @@
         return [
             remote(
                 step,
-                8 + 2 * side + end,
+                12 + 2 * side + end,
                 halo_x.at[step, end, 0 if side else cy - 1],
                 halo_y.at[step, side, end * (cx + 1)],
                 towards(name_y, size_y, me_y, side),
@@ -132,7 +142,7 @@
 
     def put_turned(field, position, value, at_x, at_y):
         entry = at_x * 3 + at_y
-        cosine, sine = phase[entry], phase[9 + entry]
+        cosine, sine = turns[0, entry : entry + 1], turns[1, entry : entry + 1]
         real, imag = value[:half], value[half:]
         put(
             field,
@@ -145,8 +155,17 @@
     def prepare(x, y):
         i = x * cy + y
         landing(x, y).wait()
-        count = counts[i]
+        count = counts[x, y]
         for s in range(slots):
+            partner = partners[x, y, s]
+            partner_x = (partner * (((1 << 20) + total_y - 1) // total_y)) >> 20
+            at_x = partner_x - me_x * cx + 1
+            at_x = jnp.where(at_x < 0, at_x + total_x, at_x)
+            at_x = jnp.where(at_x >= total_x, at_x - total_x, at_x)
+            at_y = partner - partner_x * total_y - me_y * cy + 1
+            at_y = jnp.where(at_y < 0, at_y + total_y, at_y)
+            at_y = jnp.where(at_y >= total_y, at_y - total_y, at_y)
+            table[i * slots + s] = at_x * pitch + at_y
             entry = landed[i, s] * jnp.where(s < count, 1.0, 0.0).astype(F32)
             high = entry.astype(BF16)
             weights[i, s * block : (s + 1) * block, :block] = high
@@ -157,7 +176,14 @@
     def advance(step, x, y):
         i = x * cy + y
         source = fields[step % 2]
-        lhs = jnp.concatenate([source[table[i * slots + s]] for s in range(slots)], axis=1)
+        final = (cx + 2) * pitch - 1
+        lhs = jnp.concatenate(
+            [
+                source[jnp.minimum(jnp.maximum(table[i * slots + s], 0), final)]
+                for s in range(slots)
+            ],
+            axis=1,
+        )
         product = jnp.dot(lhs, weights[i], preferred_element_type=F32)
         value = product[:width, :block] + (
             product[width:, :block] + product[:width, block:] + product[width:, block:]
@@ -187,17 +213,45 @@
         lax.fori_loop(0, count, body, 0, unroll=1 if step == 0 else 2)
 
     load_v0.wait()
-    start(x_copies(0, 1) + x_copies(0, 2) + y_copies(0) + x_copies(0, 0))
+    start(x_copies(0, ends) + y_copies(0) + x_copies(0, near) + x_copies(0, middle))
     sums[...] = jnp.zeros_like(sums)
+    row = lax.broadcasted_iota(jnp.int32, (16, block), 0)
+
+    def crossing(at, me, size):
+        low = (at == 0) & (me == 0)
+        high = (at == 2) & (me == size - 1)
+        return jnp.where(low, -1.0, jnp.where(high, 1.0, 0.0)).astype(F32)
+
+    angle = kpoint[0] * crossing(row // 3, me_x, size_x)
+    angle = angle + kpoint[1] * crossing(row % 3, me_y, size_y)
+    turns[0], turns[1] = jnp.cos(angle), jnp.sin(angle)
 
     @pl.loop(0, cx * cy)
     def _(k):
         x, y = k // cy, k % cy
         put(field_a, (x + 1) * pitch + y + 1, v0[x, y])
 
+    def put_x(step, parts):
+        for first, length in parts:
+            for y in range(first, first + length):
+                for side in range(2):
+                    put_turned(
+                        fields[step % 2],
+                        side * (cx + 1) * pitch + y + 1,
+                        halo_x[step, side, y],
+                        2 * side,
+                        1,
+                    )
+
     for step in range(STEPS):
         field = fields[step % 2]
+        more = step + 1 < STEPS
         run(step, 0)
+        if not more:
+            run(step, 5)
+        arrive(x_copies(step, ends))
+        start(corner_copies(step))
+        put_x(step, ends)
         arrive(y_copies(step))
         for side in range(2):
 
@@ -212,24 +266,8 @@
                 )
 
         run(step, 1)
-        arrive(x_copies(step, 1) + x_copies(step, 2))
-        start(corner_copies(step))
-        arrive(x_copies(step, 0))
-        for side in range(2):
-
-            @pl.loop(0, cy)
-            def _(y):
-                put_turned(
-                    field,
-                    side * (cx + 1) * pitch + y + 1,
-                    halo_x[step, side, y],
-                    2 * side,
-                    1,
-                )
-
-        run(step, 2)
-        if step + 1 < STEPS:
-            start(x_copies(step + 1, 0))
+        arrive(x_copies(step, near))
+        put_x(step, near)
         arrive(corner_copies(step))
         for side in range(2):
             for end in range(2):
@@ -240,9 +278,18 @@
                     2 * end,
                     2 * side,
                 )
+        run(step, 2)
+        if more:
+            start(x_copies(step + 1, ends) + y_copies(step + 1))
+        arrive(x_copies(step, middle))
+        put_x(step, middle)
         run(step, 3)
-        if step + 1 < STEPS:
-            start(x_copies(step + 1, 1) + x_copies(step + 1, 2) + y_copies(step + 1))
+        if more:
+            start(x_copies(step + 1, near))
+        run(step, 4)
+        if more:
+            start(x_copies(step + 1, middle))
+            run(step, 5)
 
     found = lax.dot_general(
         jnp.ones((8, block), F32),
@@ -276,8 +323,7 @@
     total[...] = found
     for step in range(STEPS):
         for copy in (
-            x_copies(step, 0) + x_copies(step, 1) + x_copies(step, 2)
-            + y_copies(step) + corner_copies(step)
+            x_copies(step, ends + near + middle) + y_copies(step) + corner_copies(step)
         ):
             copy.wait_send()
 
@@ -288,21 +334,6 @@
     slots = pair_blocks.shape[2]
     cells = cx * cy
     total_x, total_y = cx * size_x, cy * size_y
-    me_x, me_y = lax.axis_index(name_x), lax.axis_index(name_y)
-    at_x = jnp.mod(partners // total_y - me_x * cx + 1, total_x)
-    at_y = jnp.mod(partners % total_y - me_y * cy + 1, total_y)
-    table = (at_x * (cy + 2) + at_y).reshape(cells * slots)
-    side = jnp.arange(3, dtype=jnp.int32)
-
-    def crossing(me, size):
-        return jnp.where(
-            (side == 0) & (me == 0), -1, jnp.where((side == 2) & (me == size - 1), 1, 0)
-        ).astype(F32)
-
-    angle = (
-        kpoint[0] * crossing(me_x, size_x)[:, None] + kpoint[1] * crossing(me_y, size_y)[None, :]
-    ).reshape(9)
-    phase = jnp.concatenate([jnp.cos(angle), jnp.sin(angle)])
     rows = STEPS * width
     halo = (width, block)
     smem = pl.BlockSpec(memory_space=pltpu.SMEM)
@@ -330,10 +361,12 @@
             pltpu.VMEM((rows, block), F32),
             pltpu.VMEM((size_x, 8, rows), F32),
             pltpu.VMEM((size_y, 8, rows), F32),
+            pltpu.SMEM((cells * slots,), jnp.int32),
+            pltpu.VMEM((2, 16, block), F32),
             dma(()),
             dma((cells,)),
-            dma((STEPS, 12)),
-            dma((STEPS, 12)),
+            dma((STEPS, 16)),
+            dma((STEPS, 16)),
             dma((size_x,)),
             dma((size_x,)),
             dma((size_y,)),
@@ -342,7 +375,7 @@
         compiler_params=pltpu.CompilerParams(
             collective_id=0, has_side_effects=True, vmem_limit_bytes=66_000_000
         ),
-    )(table, counts.reshape(cells), phase, probes, pair_blocks)
+    )(partners, counts, kpoint, probes, pair_blocks)
     scale = 1.0 / math.sqrt(total_x * total_y * block)
     return last, (found[0] * scale).reshape(STEPS, 2, width // 2)
 

time: 66.4 us -> 55.8 us (0.84)
  Pallas kernels: 55.4 us -> 51.1 us
  local copies, waits for them, and re-layouts: 6.54 us -> 3.07 us
  other arithmetic: 3.53 us -> 0.72 us
    pallas_call x1, Pallas kernels: 55.4 us -> 51.1 us  [shards(): pl.pallas_call(functools.partial(kernel, axes), out_shape=(jax.ShapeDtype...]
    reshape x2 -> x0, local copies, waits for them, and re-layouts: 1.96 us -> none  [the longest x1 1.28 us: shards(): counts.reshape(cells)]
    slice x1 -> x0, local copies, waits for them, and re-layouts: 1.34 us -> none  [shards(): kpoint[0] * crossing(me_x, size_x)[:, None]]
    mul x1 -> x0, other arithmetic: 1.29 us -> none  [shards(): kpoint[1] * crossing(me_y, size_y)[None, :]]
    add x1 -> x0, other arithmetic: 0.8 us -> none  [shards(): table = (at_x * (cy + 2) + at_y).reshape(cells * slots)]
where the time goes in v2:
time: 55.8 us; the launch traced here: 55.5 us
  Pallas kernels  51.1 us (92%)
  local copies, waits for them, and re-layouts  3.07 us (6%)
  other arithmetic  0.72 us (1%)
  between operations  0.64 us (1%)
    pallas_call x1, Pallas kernels, shards(): pl.pallas_call(functools.partial(kernel, axes), out_shape=(jax.ShapeDtype...  51.1 us
    unnamed x1, local copies, waits for them, and re-layouts  2.41 us

profile of v2, /device:TPU:0, one launch (start us, length us, event | category | flops | bytes accessed | tf_op | source)
XLA Modules:
  0.0 55.5 jit_solution(1789553448188857623)
XLA Ops:
  0.6 51.1 %shard_map.68 = (f32[6,6,64,128]{3,2,1,0:T(8,128)}, f32[8,192]{1,0:T(8,128)}) custom-call(s32[6,6,9]{2,1,0:T(8,128)} %partners.1, s32[6,6]{1,0:T(8,128)} %counts.1, f32[2]{0:T(128)} %kpoint.1, f32[6,6,64,128]{3,2,1,0:T(8,128)} %v0_hbm.1, f32[6,6,9,128,128]{4,3,2,1,0:T(8,128)} %blocks_hbm.1), custom_call_target="tpu_custom_call" | custom-call | tf_op jit(solution)/shard_map/pallas_call | solution.py:343
  51.8 0.7 %multiply_reduce_fusion = f32[192]{0:T(256)S(1)} fusion(f32[8,192]{1,0:T(8,128)} %get-tuple-element.5), kind=kLoop, calls=%fused_computation | loop fusion | flops 192 | bytes 1536 | tf_op jit(solution)/shard_map/mul | solution.py:380
  52.5 0.7 %mul.12 = f32[3,2,32]{2,1,0:T(2,128)} reshape(f32[192]{0:T(256)S(1)} %multiply_reduce_fusion) | data formatting | bytes 1536 | tf_op jit(solution)/shard_map/mul | solution.py:380
  53.1 2.4 %copy.8 = f32[6,6,64,128]{3,2,1,0:T(8,128)} copy(f32[6,6,64,128]{3,2,1,0:T(8,128)} %get-tuple-element.8) | data formatting | bytes 2359296
